TPU v7x, 128 devices: a whole 4x4x4 slice. The times are simulated.
128 devices in a mesh: tm: 16 (over x, z_lo, core), agent: 8 (over y, z_hi).
Axes of the slice: x: 4, y: 4, z: 4 (z_hi: 2, z_lo: 2; z = z_hi * 2 + z_lo), core: 2. Of those that a mesh axis runs over, the one named last changes fastest.
Arguments:
- states: bfloat16 [96, 1024, 512], P('tm', 'agent'), may hold values from -30 to 30
- neighbours: int32 [8, 4], replicated, may hold values from 0 to 7, as said below
- w_query_t: bfloat16 [512, 512], replicated, may hold values from -16 to 16
- w_key_t: bfloat16 [512, 512], replicated, may hold values from -16 to 16
- w_value_t: bfloat16 [512, 512], replicated, may hold values from -0.25 to 0.25
- w_out_t: bfloat16 [512, 512], replicated, may hold values from -0.25 to 0.25
- w_query_a: bfloat16 [512, 512], replicated, may hold values from -16 to 16
- w_key_a: bfloat16 [512, 512], replicated, may hold values from -16 to 16
- w_value_a: bfloat16 [512, 512], replicated, may hold values from -0.25 to 0.25
- w_out_a: bfloat16 [512, 512], replicated, may hold values from -0.25 to 0.25
- w_in: bfloat16 [512, 2048], replicated, may hold values from -0.25 to 0.25
- w_mlp_out: bfloat16 [2048, 512], replicated, may hold values from -0.125 to 0.125
Outputs:
- mixed: bfloat16 [96, 1024, 512], P('tm', 'agent')
Inputs may be any that keep to these rules, and one draw needn't show every extreme that they name: neighbours[b] lists 4 different blocks, the first of them b itself.
All inputs are finite; a program needn't handle non-finite values.
Results may differ from a plain program's by a relative error of at most 0.006.
Values may be sent and summed in bfloat16 or wider, within the bound.
A program may use at most 128 MiB of HBM per device.

v0:
```python
import jax
import jax.numpy as jnp
from jax import lax
from jax.sharding import PartitionSpec as P

HEADS = 8


negative_floor = -1e30
epsilon = 1e-06


def rms_normed(values):
    wide = values.astype(jnp.float32)
    scale = lax.rsqrt(jnp.mean(wide * wide, axis=-1, keepdims=True) + epsilon)
    return (wide * scale).astype(jnp.bfloat16)


def project(normed, weight):
    return jnp.dot(normed, weight, preferred_element_type=jnp.float32).astype(jnp.bfloat16)


def attend(query, keys, values, allowed):
    batch, query_len, features = query.shape
    key_len = keys.shape[1]
    head_size = features // HEADS
    query_h = query.reshape(batch, query_len, HEADS, head_size)
    keys_h = keys.reshape(batch, key_len, HEADS, head_size)
    values_h = values.reshape(batch, key_len, HEADS, head_size)
    scores = jnp.einsum(
        "bqhe,bkhe->bhqk", query_h, keys_h, preferred_element_type=jnp.float32
    ) * head_size ** (-0.5)
    scores = jnp.where(allowed[:, None], scores, negative_floor)
    largest = jnp.max(scores, axis=-1, keepdims=True)
    weights = jnp.where(allowed[:, None], jnp.exp(scores - largest), 0.0)
    totals = jnp.sum(weights, axis=-1)
    summed = jnp.einsum(
        "bhqk,bkhe->bqhe",
        weights.astype(jnp.bfloat16),
        values_h,
        preferred_element_type=jnp.float32,
    )
    result = summed / jnp.transpose(totals, (0, 2, 1))[..., None]
    return result.reshape(batch, query_len, features).astype(jnp.bfloat16)


def local(
    states,
    neighbours,
    w_query_t,
    w_key_t,
    w_value_t,
    w_out_t,
    w_query_a,
    w_key_a,
    w_value_a,
    w_out_a,
    w_in,
    w_mlp_out,
):
    local_steps, local_agents, features = states.shape
    first_normed = rms_normed(states)
    groups = lax.axis_size("tm")
    sub_agents = local_agents // groups
    grouped = first_normed.reshape(local_steps, groups, sub_agents, features)
    sequences = lax.all_to_all(grouped, "tm", split_axis=1, concat_axis=0, tiled=True)
    full_len, single, count, width = sequences.shape
    flat = sequences.reshape(full_len, count, width)
    query = jnp.swapaxes(project(flat, w_query_t), 0, 1)
    keys = jnp.swapaxes(project(flat, w_key_t), 0, 1)
    values = jnp.swapaxes(project(flat, w_value_t), 0, 1)
    steps = jnp.arange(full_len)
    allowed = (steps[None, :] <= steps[:, None])[None]
    mixed_rows = jnp.swapaxes(attend(query, keys, values, allowed), 0, 1)
    regrouped = mixed_rows.reshape(full_len, single, count, width)
    returned = lax.all_to_all(regrouped, "tm", split_axis=0, concat_axis=1, tiled=True)
    time_mixed = returned.reshape(local_steps, local_agents, features)
    after_time = (
        states.astype(jnp.float32)
        + jnp.dot(time_mixed, w_out_t, preferred_element_type=jnp.float32)
    ).astype(jnp.bfloat16)
    second_normed = rms_normed(after_time)
    agent_query = project(second_normed, w_query_a)
    block_count = lax.axis_size("agent")
    chosen_blocks = lax.dynamic_slice_in_dim(neighbours, lax.axis_index("agent"), 1, 0)[0]
    neighbour_count = neighbours.shape[1]
    everyone = lax.all_gather(second_normed, "agent", axis=1, tiled=True)
    picked = jnp.take(
        everyone.reshape(local_steps, block_count, local_agents, features), chosen_blocks, axis=1
    )
    picked = picked.reshape(local_steps, neighbour_count * local_agents, features)
    agent_key = project(picked, w_key_a)
    agent_value = project(picked, w_value_a)
    allowed_all = jnp.ones((1, local_agents, neighbour_count * local_agents), dtype=bool)
    agent_mixed = attend(agent_query, agent_key, agent_value, allowed_all)
    after_agent = (
        after_time.astype(jnp.float32)
        + jnp.dot(agent_mixed, w_out_a, preferred_element_type=jnp.float32)
    ).astype(jnp.bfloat16)
    inner = jax.nn.gelu(
        jnp.dot(rms_normed(after_agent), w_in, preferred_element_type=jnp.float32), approximate=True
    ).astype(jnp.bfloat16)
    final = after_agent.astype(jnp.float32) + jnp.dot(
        inner, w_mlp_out, preferred_element_type=jnp.float32
    )
    return final.astype(jnp.bfloat16)


def solution(mesh):
    placed = (P("tm", "agent", None), P(), P(), P(), P(), P(), P(), P(), P(), P(), P(), P())
    return jax.shard_map(
        local, mesh=mesh, in_specs=placed, out_specs=P("tm", "agent", None), check_vma=False
    )
```

profile of v0, /device:TPU:1, one launch (start us, length us, event | category | flops | bytes accessed | tf_op | source)
XLA Modules:
  0.0 202.4 jit_solution(6569923410011839906)
XLA Ops:
  6.5 0.0 copy-start
  6.5 1.5 fusion.26
  8.1 1.4 fusion.53
  9.4 1.0 copy.36
  10.4 7.2 %all-to-all-start = ((bf16[6,16,8,512]{3,2,0,1:T(8,128)(2,1)}), bf16[6,16,8,512]{3,2,0,1:T(8,128)(2,1)S(1)}, u32[]{:S(2)}, u32[]{:S(2)}) async-start(bf16[6,16,8,512]{3,2,0,1:T(8,128)(2,1)} %copy.36), calls=%async_computation | async-start | bytes 1572864 | tf_op jit(solution)/shard_map/all_to_all | solution.py:66
  17.6 0.0 all-gather.2.cloned.1.call-start
  17.6 12.6 %all-to-all-done = bf16[6,16,8,512]{3,2,0,1:T(8,128)(2,1)S(1)} async-done(((bf16[6,16,8,512]{3,2,0,1:T(8,128)(2,1)}), bf16[6,16,8,512]{3,2,0,1:T(8,128)(2,1)S(1)}, u32[]{:S(2)}, u32[]{:S(2)}) %all-to-all-start) | async-done | bytes 786464 | tf_op jit(solution)/shard_map/all_to_all | solution.py:66
  30.2 0.9 copy-done.3
  31.1 2.5 %fusion.50 = bf16[8,96,512]{2,0,1:T(8,128)(2,1)} fusion(bf16[96,8,512]{2,1,0:T(8,128)(2,1)S(1)} %bitcast.119, bf16[512,512]{1,0:T(8,128)(2,1)} %param.15), kind=kOutput, calls=%fused_computation.60 | convolution fusion | flops 403046400 | bytes 2097152 | tf_op jit(solution)/shard_map/dot_general | solution.py:20
  33.6 1.8 copy.39
  35.4 2.7 %fusion.49 = bf16[8,96,512]{2,0,1:T(8,128)(2,1)} fusion(bf16[96,8,512]{2,1,0:T(8,128)(2,1)} %bitcast.120, bf16[512,512]{1,0:T(8,128)(2,1)} %param.14), kind=kOutput, calls=%fused_computation.59 | convolution fusion | flops 403046400 | bytes 2097152 | tf_op jit(solution)/shard_map/dot_general | solution.py:20
  38.1 2.8 %fusion.48 = bf16[8,96,512]{2,0,1:T(8,128)(2,1)} fusion(bf16[96,8,512]{2,1,0:T(8,128)(2,1)} %bitcast.121, bf16[512,512]{1,0:T(8,128)(2,1)} %param.16), kind=kOutput, calls=%fused_computation.58 | convolution fusion | flops 403046400 | bytes 2097152 | tf_op jit(solution)/shard_map/dot_general | solution.py:20
  40.9 2.5 %copy.37 = bf16[8,96,512]{1,2,0:T(8,128)(2,1)} copy(bf16[8,96,512]{2,0,1:T(8,128)(2,1)} %fusion.48) | data formatting | bytes 1572864 | tf_op jit(solution)/shard_map/convert_element_type | solution.py:20
  43.4 2.5 %copy.38 = bf16[8,96,512]{1,2,0:T(8,128)(2,1)} copy(bf16[8,96,512]{2,0,1:T(8,128)(2,1)} %fusion.49) | data formatting | bytes 1572864 | tf_op jit(solution)/shard_map/convert_element_type | solution.py:20
  45.8 4.0 %fusion.76 = (f32[8,8,96]{2,1,0:T(8,128)S(1)}, bf16[8,8,96,96]{2,3,1,0:T(8,128)(2,1)}) fusion(pred[96,96]{0,1:T(8,128)(4,1)S(1)} %iota_compare_fusion, bf16[8,96,8,64]{1,3,2,0:T(8,128)(2,1)} %bitcast.117, bf16[8,96,8,64]{1,3,2,0:T(8,128)(2,1)S(1)} %bitcast.115), kind=kOutput, calls=%fused_computation.92 | convolution fusion | flops 79036512 | bytes 2786304 | tf_op jit(solution)/shard_map/sub | solution.py:35
  49.9 3.3 %fusion.21 = bf16[8,96,8,64]{1,3,2,0:T(8,128)(2,1)} fusion(bf16[8,96,8,64]{1,3,2,0:T(8,128)(2,1)} %bitcast.116, bf16[8,8,96,96]{2,3,1,0:T(8,128)(2,1)} %get-tuple-element.6, f32[8,96,8]{1,2,0:T(8,128)S(1)} %bitcast.126), kind=kOutput, calls=%fused_computation.38 | convolution fusion | flops 76283904 | bytes 2777088 | tf_op jit(solution)/shard_map/bhqk,bkhe->bqhe/dot_general | solution.py:37
  53.1 1.8 copy.41
  54.9 16.6 %all_to_all.30 = bf16[96,1,8,512]{3,2,1,0:T(8,128)(2,1)S(1)} all-to-all(bf16[96,1,8,512]{3,2,1,0:T(8,128)(2,1)S(1)} %bitcast.113), channel_id=1, replica_groups=mesh['tm'=16,'agent'=8] {'tm'}, dimensions={0} | all-to-all | bytes 1572864 | tf_op jit(solution)/shard_map/all_to_all | solution.py:76
  71.6 0.0 copy-done.6
  71.6 1.9 fusion.29
  73.4 0.0 copy-start.1
  73.5 0.9 copy-done.1
  74.3 1.1 fusion.30
  75.5 0.0 all-gather.2.cloned.1.call-update
  75.5 0.0 copy-done.5
  75.5 0.2 dynamic-slice_reduce_fusion
  75.7 0.1 broadcast_bitcast_fusion
  75.8 0.0 copy-done.7
  75.8 2.6 %convolution_convert_fusion.2 = bf16[6,128,512]{2,1,0:T(8,128)(2,1)} fusion(bf16[6,128,512]{2,1,0:T(8,128)(2,1)} %fusion.30, bf16[512,512]{1,0:T(8,128)(2,1)S(1)} %copy-done.7), kind=kOutput, calls=%fused_computation.54 | convolution fusion | flops 403046400 | bytes 2097152 | tf_op jit(solution)/shard_map/dot_general | solution.py:20
  78.4 1.5 copy.45
  79.9 85.0 %all-gather.2.cloned.1.call-done = bf16[6,1024,512]{2,1,0:T(8,128)(2,1)} async-done(((bf16[6,128,512]{2,1,0:T(8,128)(2,1)}), bf16[6,1024,512]{2,1,0:T(8,128)(2,1)}) %all-gather.2.cloned.1.call-update) | async-done | bytes 6291472 | tf_op jit(solution)/shard_map/all_gather | solution.py:87
  164.8 5.2 %gather_fusion = bf16[4,6,128,512]{3,2,1,0:T(8,128)(2,1)} fusion(bf16[6,8,128,512]{3,2,1,0:T(8,128)(2,1)} %bitcast.114, s32[1024]{0:T(1024)S(1)} %pad_clamp_fusion), kind=kCustom, calls=%fused_computation | custom fusion | bytes 6291472 | tf_op jit(solution)/shard_map/jit(_take)/gather | solution.py:88
  170.1 2.1 %copy.43 = bf16[6,4,128,512]{3,2,1,0:T(8,128)(2,1)S(1)} copy(bf16[6,4,128,512]{3,2,0,1:T(8,128)(2,1)} %bitcast.110) | data formatting | bytes 6291456 | tf_op jit(solution)/shard_map/jit(_take)/gather | solution.py:88
  172.2 0.0 copy-start.8
  172.2 0.6 bitcast_select_fusion
  172.8 0.4 copy-done.8
  173.2 1.9 convolution_convert_fusion
  175.1 0.0 copy-done.9
  175.1 3.6 %convolution_convert_fusion.1 = bf16[6,512,512]{1,2,0:T(8,128)(2,1)} fusion(bf16[6,512,512]{2,1,0:T(8,128)(2,1)S(1)} %bitcast_select_fusion, bf16[512,512]{1,0:T(8,128)(2,1)S(1)} %copy-done.9), kind=kOutput, calls=%fused_computation.33 | convolution fusion | flops 1612185600 | bytes 6815744 | tf_op jit(solution)/shard_map/dot_general | solution.py:20
  178.7 2.0 multiply_reduce_fusion
  180.7 3.1 %fusion.1 = f32[6,8,128]{2,1,0:T(8,128)S(1)} fusion(f32[6,8,128,512]{3,2,1,0:T(8,128)S(1)} %get-tuple-element.10, f32[6,8,128]{2,1,0:T(8,128)S(1)} %get-tuple-element.9), kind=kLoop, calls=%fused_computation.4 | loop fusion | flops 9431040 | bytes 12632064 | tf_op jit(solution)/shard_map/reduce_sum | solution.py:36
  183.8 0.0 copy-start.2
  183.8 0.0 copy-start.4
  183.8 4.9 %fusion.35 = bf16[6,128,8,64]{1,3,2,0:T(8,128)(2,1)S(1)} fusion(bf16[6,512,8,64]{1,3,2,0:T(8,128)(2,1)} %bitcast.125, f32[6,8,128,512]{3,2,1,0:T(8,128)S(1)} %get-tuple-element.10, f32[6,8,128]{2,1,0:T(8,128)S(1)} %get-tuple-element.9, f32[6,128,8]{1,2,0:T(8,128)S(1)} %bitcast.124), kind=kOutput, calls=%fused_computation.49 | convolution fusion | flops 412876800 | bytes 16564224 | tf_op jit(solution)/shard_map/bhqk,bkhe->bqhe/dot_general | solution.py:37
  188.7 0.0 copy-done.2
  188.7 0.0 copy-done.4
  188.7 0.7 fusion.32
  189.4 6.1 %fusion.34 = bf16[6,128,512]{2,1,0:T(8,128)(2,1)} fusion(bf16[6,128,512]{2,1,0:T(8,128)(2,1)S(1)} %get-tuple-element.12, bf16[2048,512]{1,0:T(8,128)(2,1)S(1)} %copy-done, bf16[512,2048]{1,0:T(8,128)(2,1)} %param.22, f32[6,128]{1,0:T(8,128)S(1)} %add_rsqrt_fusion), kind=kOutput, calls=%fused_computation.47 | convolution fusion | flops 3237740544 | bytes 5770240 | tf_op jit(solution)/shard_map/dot_general | solution.py:103
  (13 shorter events, 0.1 us)
Async XLA Ops:
  6.5 182.9 %copy-start = (bf16[2048,512]{1,0:T(8,128)(2,1)S(1)}, bf16[2048,512]{1,0:T(8,128)(2,1)}, u32[]{:S(2)}) copy-start(bf16[2048,512]{1,0:T(8,128)(2,1)} %param.23) | copy-start | bytes 6291460
  10.4 19.8 %all-to-all-start = ((bf16[6,16,8,512]{3,2,0,1:T(8,128)(2,1)}), bf16[6,16,8,512]{3,2,0,1:T(8,128)(2,1)S(1)}, u32[]{:S(2)}, u32[]{:S(2)}) async-start(bf16[6,16,8,512]{3,2,0,1:T(8,128)(2,1)} %copy.36), calls=%async_computation | async-start | bytes 1572864 | tf_op jit(solution)/shard_map/all_to_all | solution.py:66
  17.6 147.3 %all-gather.2.cloned.1.call-start = ((), (), s32[]{:S(2)}) async-start(), calls=%async_computation.2 | async-start | bytes 7077888 | tf_op jit(solution)/shard_map/all_gather | solution.py:87
  30.2 0.9 copy-start.3
  53.1 18.4 %copy-start.6 = (bf16[512,512]{1,0:T(8,128)(2,1)S(1)}, bf16[512,512]{1,0:T(8,128)(2,1)}, u32[]{:S(2)}) copy-start(bf16[512,512]{1,0:T(8,128)(2,1)} %param.17) | copy-start | bytes 1572868
  71.6 3.9 %copy-start.5 = (s32[8,4]{0,1:T(4,128)S(1)}, s32[8,4]{0,1:T(4,128)}, u32[]{:S(2)}) copy-start(s32[8,4]{0,1:T(4,128)} %param.13) | copy-start | bytes 388
  71.6 4.2 %copy-start.7 = (bf16[512,512]{1,0:T(8,128)(2,1)S(1)}, bf16[512,512]{1,0:T(8,128)(2,1)}, u32[]{:S(2)}) copy-start(bf16[512,512]{1,0:T(8,128)(2,1)} %param.18) | copy-start | bytes 1572868
  73.4 0.9 copy-start.1
  172.2 1.0 copy-start.8
  173.2 1.9 copy-start.9
  183.8 4.9 %copy-start.2 = (bf16[6,128,512]{2,1,0:T(8,128)(2,1)S(1)}, bf16[6,128,512]{2,1,0:T(8,128)(2,1)}, u32[]{:S(2)}) copy-start(bf16[6,128,512]{2,1,0:T(8,128)(2,1)} %copy-done.1) | copy-start | bytes 2359300
  183.8 4.9 %copy-start.4 = (bf16[512,512]{1,0:T(8,128)(2,1)S(1)}, bf16[512,512]{1,0:T(8,128)(2,1)}, u32[]{:S(2)}) copy-start(bf16[512,512]{1,0:T(8,128)(2,1)} %param.21) | copy-start | bytes 1572868
Sparse Core Ops, SparseCore 0:
  75.6 89.1 all-gather.1
where the time goes:
time: 203 us; the launch traced here: 202 us
  waiting for transfers between devices  97.6 us (48%)
  matrix products  38.9 us (19%)
  local copies, waits for them, and re-layouts  20.7 us (10%)
  blocking collectives  16.6 us (8%)
  between operations  13.6 us (7%)
  other arithmetic  7.73 us (4%)
  starting transfers between devices  7.21 us (4%)
    all_gather x1, waiting for transfers between devices, local(): everyone = lax.all_gather(second_normed, 'agent', axis=1, tiled=True)  85 us
    all_to_all x1, blocking collectives, local(): lax.all_to_all(regrouped, 'tm', split_axis=0, concat_axis=1, tiled=True)  16.6 us
    dot_general x6, matrix products, project(): jnp.dot(normed, weight, preferred_element_type=jnp.float32)  16 us
    all_to_all x1, waiting for transfers between devices, local(): lax.all_to_all(grouped, 'tm', split_axis=1, concat_axis=0, tiled=True)  12.6 us
    convert_element_type x4, local copies, waits for them, and re-layouts, project(): jnp.dot(normed, weight, preferred_element_type=jnp.float32)  8.2 us
    dot_general x2, matrix products, attend(): jnp.einsum('bhqk,bkhe->bqhe', weights.astype(jnp.bfloat16), values_h, pre...  8.14 us
    gather x2, local copies, waits for them, and re-layouts, local(): jnp.take(everyone.reshape(local_steps, block_count, local_agents, feature...  7.32 us
    all_to_all x1, starting transfers between devices, local(): lax.all_to_all(grouped, 'tm', split_axis=1, concat_axis=0, tiled=True)  7.17 us
  transfers between devices with their start and end apart: 2, of which 2 were waited for; matrix products, arithmetic and copies ran while one was open for 2% of the time, Pallas kernels for 0%

commit v1 on v0

v1 whole, which is shorter than its diff:
```python
import functools

import jax
import jax.numpy as jnp
from jax import lax
from jax.experimental import pallas as pl
from jax.experimental.pallas import tpu as pltpu
from jax.sharding import PartitionSpec as P

MESH = pl.DeviceIdType.MESH
HEADS = 8
epsilon = 1e-06
negative_floor = -1e30
bf16 = jnp.bfloat16
f32 = jnp.float32


def normed(wide):
    return (wide * lax.rsqrt(jnp.mean(wide * wide, axis=-1, keepdims=True) + epsilon)).astype(bf16)


def mm(a, b):
    return jnp.dot(a, b, preferred_element_type=f32)


def mm_nt(a, b):
    return lax.dot_general(a, b, (((1,), (1,)), ((), ())), preferred_element_type=f32)


def two_heads(query):
    low = lax.broadcasted_iota(jnp.int32, query.shape, 1) < 64
    none = jnp.zeros_like(query)
    return jnp.concatenate([jnp.where(low, query, none), jnp.where(low, none, query)], axis=0)


def join_heads(stacked):
    n = stacked.shape[0] // 2
    low = lax.broadcasted_iota(jnp.int32, (n, 128), 1) < 64
    return jnp.where(low, stacked[:n], stacked[n:])


def kernel(
    groups, blocks, steps, agents, near,
    states_hbm, nb_ref, wqt_hbm, wkt_hbm, wvt_hbm, wot_hbm, wqa_hbm, wka_hbm, wva_hbm, woa_hbm, win_hbm, wmo_hbm,
    out_hbm,
    states, wide, wqt, wkt, wvt, wot, wqa, wka, wva, woa, win, wmo,
    send1, recv1, qf, kf, vf, mask, mixed_t, send2, recv2, after, aft_b, qkv, ret, am, outs,
    in_sem, out_sem, s1, r1, s2, r2, s3, r3, s4, r4, self3, self4, *recv3,
):
    tm = lax.axis_index("tm")
    ag = lax.axis_index("agent")
    sub = agents // groups
    rows = steps * sub
    half_steps = steps // 2
    pairs = HEADS // 2

    def tm_peer(k):
        return lax.rem(tm + k + groups, groups)

    def ag_peer(k):
        return lax.rem(ag + k + blocks, blocks)

    loads = [
        pltpu.make_async_copy(source, target, in_sem.at[n])
        for n, (source, target) in enumerate(
            [(states_hbm, states), (wqt_hbm, wqt), (wkt_hbm, wkt), (wvt_hbm, wvt), (wot_hbm, wot), (wqa_hbm, wqa),
             (wka_hbm, wka), (wva_hbm, wva), (woa_hbm, woa), (win_hbm, win), (wmo_hbm, wmo)]
        )
    ]
    for load in loads:
        load.start()
    barrier = pltpu.get_barrier_semaphore()
    for k in range(1, groups):
        pl.semaphore_signal(barrier, inc=1, device_id={"tm": tm_peer(k)}, device_id_type=MESH)
    for k in range(1, blocks):
        pl.semaphore_signal(barrier, inc=1, device_id={"agent": ag_peer(k)}, device_id_type=MESH)

    loads[0].wait()
    wide[...] = states[...].astype(f32)
    pl.semaphore_wait(barrier, groups + blocks - 2)

    first = []
    for k in list(range(1, groups)) + [0]:
        base = pl.multiple_of(tm_peer(k) * sub, sub)
        piece = jnp.concatenate([wide[t, pl.ds(base, sub), :] for t in range(steps)], axis=0).astype(bf16)
        if k == 0:
            recv1[0] = piece
            continue
        send1[k] = piece
        copy = pltpu.make_async_remote_copy(
            src_ref=send1.at[k], dst_ref=recv1.at[k], send_sem=s1.at[k], recv_sem=r1.at[k],
            device_id={"tm": tm_peer(k)}, device_id_type=MESH,
        )
        copy.start()
        first.append(copy)

    total_steps = groups * steps

    def times(shape, axis):
        row = lax.broadcasted_iota(jnp.int32, shape, axis).astype(f32)
        row = jnp.where(row >= total_steps, row - total_steps, row)
        slot = jnp.floor((row + 0.5) / steps)
        owner = tm.astype(f32) - slot
        owner = jnp.where(owner < 0, owner + groups, owner)
        return row + steps * (owner - slot)

    shape = (2 * total_steps, total_steps)
    mask[...] = jnp.where(times(shape, 1) <= times(shape, 0), 0.0, negative_floor)

    for load in loads[1:4]:
        load.wait()
    batch = 4
    for g in range(groups // batch):
        for k in range(g * batch, (g + 1) * batch):
            if k:
                first[k - 1].wait_recv()
        there = pl.ds(g * batch * rows, batch * rows)
        flat = normed(recv1[g * batch:(g + 1) * batch].reshape(batch * rows, 512).astype(f32))
        for target, weight, scale in ((qf, wqt, 0.125), (kf, wkt, None), (vf, wvt, None)):
            result = mm(flat, weight[...])
            if scale is not None:
                result = result * scale
            for h in range(pairs):
                target[h, there, :] = result[:, h * 128:(h + 1) * 128]

    def one_agent(a, carry):
        mine = pl.ds(a, total_steps, stride=sub)
        for h in range(pairs):
            query = two_heads(qf[h, mine, :].astype(bf16))
            scores = mm_nt(query, kf[h, mine, :].astype(bf16)) + mask[...]
            weights = jnp.exp(scores - jnp.max(scores, axis=-1, keepdims=True))
            totals = jnp.sum(weights, axis=-1, keepdims=True)
            summed = mm(weights.astype(bf16), vf[h, mine, :].astype(bf16))
            mixed_t[h, mine, :] = join_heads(summed / totals)
        return carry

    lax.fori_loop(0, sub, one_agent, 0)

    second = []
    for k in list(range(1, groups)) + [0]:
        piece = jnp.concatenate([mixed_t[h, pl.ds(k * rows, rows), :] for h in range(pairs)], axis=1).astype(bf16)
        if k == 0:
            recv2[0] = piece
            continue
        send2[k] = piece
        copy = pltpu.make_async_remote_copy(
            src_ref=send2.at[k], dst_ref=recv2.at[k], send_sem=s2.at[k], recv_sem=r2.at[k],
            device_id={"tm": tm_peer(-k)}, device_id_type=MESH,
        )
        copy.start()
        second.append(copy)

    loads[4].wait()
    for g in range(groups // batch):
        for k in range(g * batch, (g + 1) * batch):
            if k:
                second[k - 1].wait_recv()
        added = mm(recv2[g * batch:(g + 1) * batch].reshape(batch * rows, 512), wot[...])
        for k in range(batch):
            base = pl.multiple_of(tm_peer(g * batch + k) * sub, sub)
            for t in range(steps):
                after[t, pl.ds(base, sub), :] = added[(k * steps + t) * sub:(k * steps + t + 1) * sub]

    for load in loads[5:8]:
        load.wait()
    my_half = ag // pairs
    my_pair = lax.rem(ag, pairs)
    my_lanes = pl.ds(pl.multiple_of(my_pair * 128, 128), 128)
    third = []
    for t in range(half_steps):
        both = [
            (wide[t + h * half_steps] + after[t + h * half_steps]).astype(bf16) for h in range(2)
        ]
        for h in range(2):
            aft_b[t + h * half_steps] = both[h]
        flat = normed(jnp.concatenate(both, axis=0).astype(f32))
        for n, (weight, scale) in enumerate([(wqa, 0.125), (wka, 1.0), (wva, 1.0)]):
            result = mm(flat, weight[...])
            if n == 0:
                result = result * scale
            result = result.astype(bf16)
            for h in range(2):
                qkv[t, h, n] = result[h * agents:(h + 1) * agents]
        for k in range(1, blocks):
            peer = ag_peer(k)
            lanes = pl.ds(pl.multiple_of(lax.rem(peer, pairs) * 128, 128), 128)
            copy = pltpu.make_async_remote_copy(
                src_ref=qkv.at[t, peer // pairs, :, :, lanes], dst_ref=recv3[t].at[k],
                send_sem=s3.at[t, k], recv_sem=r3.at[t, k],
                device_id={"agent": peer}, device_id_type=MESH,
            )
            copy.start()
            third.append(copy)
        own = pltpu.make_async_copy(qkv.at[t, my_half, :, :, my_lanes], recv3[t].at[0], self3.at[t])
        own.start()
        third.append(own)

    fourth = []

    def attention(t):
        for copy in third[t * blocks:(t + 1) * blocks - 1]:
            copy.wait_recv()
        third[(t + 1) * blocks - 1].wait()

        def one_block(k, carry):
            block = ag_peer(-k)
            query = two_heads(recv3[t][k, 0])
            slots = [lax.rem(ag - nb_ref[block, j] + blocks, blocks) for j in range(near)]
            keys = jnp.concatenate([recv3[t][slot, 1] for slot in slots], axis=0)
            values = jnp.concatenate([recv3[t][slot, 2] for slot in slots], axis=0)
            scores = mm_nt(query, keys)
            weights = jnp.exp(scores - jnp.max(scores, axis=-1, keepdims=True))
            totals = jnp.sum(weights, axis=-1, keepdims=True)
            summed = mm(weights.astype(bf16), values)
            ret[t, k] = join_heads(summed / totals).astype(bf16)
            return carry

        lax.fori_loop(0, blocks, one_block, 0)
        target = am.at[my_half * half_steps + t, :, my_lanes]
        for k in range(1, blocks):
            copy = pltpu.make_async_remote_copy(
                src_ref=ret.at[t, k], dst_ref=target, send_sem=s4.at[t, k], recv_sem=r4.at[t, k],
                device_id={"agent": ag_peer(-k)}, device_id_type=MESH,
            )
            copy.start()
            fourth.append(copy)
        own = pltpu.make_async_copy(ret.at[t, 0], target, self4.at[t])
        own.start()
        fourth.append(own)

    stores = []

    def tail(t):
        for copy in fourth[t * blocks:(t + 1) * blocks - 1]:
            copy.wait_recv()
        fourth[(t + 1) * blocks - 1].wait()
        where = [t, t + half_steps]
        both = jnp.concatenate([am[w] for w in where], axis=0)
        base = jnp.concatenate([aft_b[w] for w in where], axis=0).astype(f32)
        after_agent = (base + mm(both, woa[...])).astype(bf16).astype(f32)
        inner = jax.nn.gelu(mm(normed(after_agent), win[...]), approximate=True).astype(bf16)
        final = (after_agent + mm(inner, wmo[...])).astype(bf16)
        for n, w in enumerate(where):
            outs[w] = final[n * agents:(n + 1) * agents]
            store = pltpu.make_async_copy(outs.at[w], out_hbm.at[w], out_sem.at[w])
            store.start()
            stores.append(store)

    attention(0)
    for load in loads[8:]:
        load.wait()
    for t in range(1, half_steps):
        attention(t)
        tail(t - 1)
    tail(half_steps - 1)

    for copy in first + second:
        copy.wait_send()
    for t in range(half_steps):
        for copy in third[t * blocks:(t + 1) * blocks - 1] + fourth[t * blocks:(t + 1) * blocks - 1]:
            copy.wait_send()
    for store in stores:
        store.wait()


def local(
    groups, blocks,
    states, neighbours, w_query_t, w_key_t, w_value_t, w_out_t, w_query_a, w_key_a, w_value_a, w_out_a, w_in, w_mlp_out,
):
    steps, agents, width = states.shape
    hidden = w_in.shape[1]
    rows = steps * (agents // groups)
    total = groups * steps
    square = (width, width)
    half = steps // 2
    anywhere = pl.BlockSpec(memory_space=pl.ANY)
    dma = pltpu.SemaphoreType.DMA
    return pl.pallas_call(
        functools.partial(kernel, groups, blocks, steps, agents, neighbours.shape[1]),
        out_shape=jax.ShapeDtypeStruct(states.shape, bf16),
        in_specs=[anywhere, pl.BlockSpec(memory_space=pltpu.SMEM)] + [anywhere] * 10,
        out_specs=anywhere,
        scratch_shapes=[
            pltpu.VMEM(states.shape, bf16),
            pltpu.VMEM(states.shape, f32),
            *[pltpu.VMEM(square, bf16)] * 8,
            pltpu.VMEM((width, hidden), bf16),
            pltpu.VMEM((hidden, width), bf16),
            pltpu.VMEM((groups, rows, width), bf16),
            pltpu.VMEM((groups, rows, width), bf16),
            *[pltpu.VMEM((width // 128, groups * rows, 128), f32)] * 3,
            pltpu.VMEM((2 * total, total), f32),
            pltpu.VMEM((width // 128, groups * rows, 128), f32),
            pltpu.VMEM((groups, rows, width), bf16),
            pltpu.VMEM((groups, rows, width), bf16),
            pltpu.VMEM(states.shape, f32),
            pltpu.VMEM(states.shape, bf16),
            pltpu.VMEM((half, 2, 3, agents, width), bf16),
            pltpu.VMEM((half, blocks, agents, 128), bf16),
            pltpu.VMEM(states.shape, bf16),
            pltpu.VMEM(states.shape, bf16),
            dma((11,)), dma((steps,)),
            dma((groups,)), dma((groups,)), dma((groups,)), dma((groups,)),
            dma((half, blocks)), dma((half, blocks)), dma((half, blocks)), dma((half, blocks)),
            dma((half,)), dma((half,)),
            *[pltpu.VMEM((blocks, 3, agents, 128), bf16)] * half,
        ],
        compiler_params=pltpu.CompilerParams(
            collective_id=0, has_side_effects=True, vmem_limit_bytes=60 * 1024 * 1024
        ),
    )(states, neighbours, w_query_t, w_key_t, w_value_t, w_out_t, w_query_a, w_key_a, w_value_a, w_out_a, w_in, w_mlp_out)


def solution(mesh):
    placed = (P("tm", "agent", None), P(), P(), P(), P(), P(), P(), P(), P(), P(), P(), P())
    return jax.shard_map(
        functools.partial(local, mesh.shape["tm"], mesh.shape["agent"]),
        mesh=mesh, in_specs=placed, out_specs=P("tm", "agent", None), check_vma=False,
    )
```

time: 203 us -> 96.1 us (0.47)
  the two profiles are of different devices: /device:TPU:1 before, /device:TPU:28 now
where the time goes in v1:
time: 96.1 us; the launch traced here: 95.9 us
  Pallas kernels  92.4 us (96%)
  local copies, waits for them, and re-layouts  3.44 us (4%)
    pallas_call x1, Pallas kernels, local(): pl.pallas_call(functools.partial(kernel, groups, blocks, steps, agents, n...  92.4 us
    unnamed x2, local copies, waits for them, and re-layouts  3.44 us

profile of v1, /device:TPU:28, one launch (start us, length us, event | category | flops | bytes accessed | tf_op | source)
XLA Modules:
  0.0 95.9 jit_solution(1982737701728422365)
XLA Ops:
  0.0 1.3 %copy.13.nb_ref = s32[8,4]{1,0:T(8,128)} copy(s32[8,4]{0,1:T(4,128)} %param.13) | data formatting | bytes 256 | tf_op args[1]
  1.3 92.4 %shard_map.118 = bf16[6,128,512]{2,1,0:T(8,128)(2,1)} custom-call(bf16[6,128,512]{2,1,0:T(8,128)(2,1)} %states_hbm.1, s32[8,4]{1,0:T(8,128)} %copy.13.nb_ref, bf16[512,512]{1,0:T(8,128)(2,1)} %wqt_hbm.1, bf16[512,512]{1,0:T(8,128)(2,1)} %wkt_hbm.1, bf16[512,512]{1,0:T(8,128)(2,1)} %wvt_hbm.1, bf16[512,512]{1,0:T(8,128)(2,1)} %wot_hbm.1, ...), custom_call_target="tpu_custom_call" | custom-call | tf_op jit(solution)/shard_map/pallas_call | solution.py:278
  93.8 2.1 %copy.15 = bf16[6,128,512]{2,1,0:T(8,128)(2,1)} copy(bf16[6,128,512]{2,1,0:T(8,128)(2,1)} %shard_map.118) | data formatting | bytes 1572864

commit v2 on v1

v2 whole, which is shorter than its diff:
```python
import functools

import jax
import jax.numpy as jnp
from jax import lax
from jax.experimental import pallas as pl
from jax.experimental.pallas import tpu as pltpu
from jax.sharding import PartitionSpec as P

MESH = pl.DeviceIdType.MESH
HEADS = 8
epsilon = 1e-06
negative_floor = -1e30
bf16 = jnp.bfloat16
f32 = jnp.float32


def normed(wide):
    return (wide * lax.rsqrt(jnp.mean(wide * wide, axis=-1, keepdims=True) + epsilon)).astype(bf16)


def mm(a, b):
    return jnp.dot(a, b, preferred_element_type=f32)


def mm_nt(a, b):
    return lax.dot_general(a, b, (((1,), (1,)), ((), ())), preferred_element_type=f32)


def two_heads(query):
    low = lax.broadcasted_iota(jnp.int32, query.shape, 1) < 64
    none = jnp.zeros_like(query)
    return jnp.concatenate([jnp.where(low, query, none), jnp.where(low, none, query)], axis=0)


def join_heads(stacked):
    n = stacked.shape[0] // 2
    low = lax.broadcasted_iota(jnp.int32, (n, 128), 1) < 64
    return jnp.where(low, stacked[:n], stacked[n:])


def kernel(
    groups, blocks, steps, agents, near,
    states_hbm, nb_hbm, wqt_hbm, wkt_hbm, wvt_hbm, wot_hbm, wqa_hbm, wka_hbm, wva_hbm, woa_hbm, win_hbm, wmo_hbm,
    out_hbm,
    nb_ref, states, wide, wqt, wkt, wvt, wot, wqa, wka, wva, wqb, wkb, wvb, woa, win, wmo,
    send1, recv1, qf, kf, vf, mask, mixed_t, send2, recv2, after, aft_b, tokens, all_full, all_part,
    qkv_full, qkv_part, ret_full, ret_part, am, outs,
    in_sem, out_sem, s1, r1, s2, r2, s3, r3, s4, r4, s5, r5,
):
    tm = lax.axis_index("tm")
    ag = lax.axis_index("agent")
    core = lax.rem(tm, 2)
    sub = agents // groups
    rows = steps * sub
    pairs = HEADS // 2
    half = agents // 2

    def tm_peer(k):
        return lax.rem(tm + k + groups, groups)

    def ag_peer(k):
        return lax.rem(ag + k + blocks, blocks)

    duo, side = ag // 2, lax.rem(ag, 2)
    full_core, full_step = side, duo
    part_core, part_step = duo // 2, 4 + lax.rem(duo, 2)
    full_lanes = pl.ds(pl.multiple_of(core * 256, 256), 256)
    part_lanes = pl.ds(pl.multiple_of((side * 2 + core) * 128, 128), 128)

    sources = [(states_hbm, states), (nb_hbm, nb_ref), (wqt_hbm, wqt), (wkt_hbm, wkt), (wvt_hbm, wvt), (wot_hbm, wot)]
    for hbm, wide_cols, few_cols in ((wqa_hbm, wqa, wqb), (wka_hbm, wka, wkb), (wva_hbm, wva, wvb)):
        sources += [(hbm.at[:, full_lanes], wide_cols), (hbm.at[:, part_lanes], few_cols)]
    sources += [(woa_hbm, woa), (win_hbm, win), (wmo_hbm, wmo)]
    loads = [pltpu.make_async_copy(source, target, in_sem.at[n]) for n, (source, target) in enumerate(sources)]
    loads[0].start()
    barrier = pltpu.get_barrier_semaphore()
    for k in range(1, groups):
        pl.semaphore_signal(barrier, inc=1, device_id={"tm": tm_peer(k)}, device_id_type=MESH)
    for k in range(1, blocks):
        for c in range(2):
            pl.semaphore_signal(
                barrier, inc=1, device_id={"tm": tm - core + c, "agent": ag_peer(k)}, device_id_type=MESH
            )
    for load in loads[1:]:
        load.start()

    loads[0].wait()
    wide[...] = states[...].astype(f32)
    for k in range(groups):
        base = pl.multiple_of(tm_peer(k) * sub, sub)
        piece = jnp.concatenate([wide[t, pl.ds(base, sub), :] for t in range(steps)], axis=0).astype(bf16)
        if k == 0:
            recv1[0] = piece
        else:
            send1[k] = piece
    pl.semaphore_wait(barrier, groups - 1 + 2 * (blocks - 1))
    first = []
    for k in range(1, groups):
        copy = pltpu.make_async_remote_copy(
            src_ref=send1.at[k], dst_ref=recv1.at[k], send_sem=s1.at[k], recv_sem=r1.at[k],
            device_id={"tm": tm_peer(k)}, device_id_type=MESH,
        )
        copy.start()
        first.append(copy)

    total_steps = groups * steps

    def times(shape, axis):
        row = lax.broadcasted_iota(jnp.int32, shape, axis).astype(f32)
        row = jnp.where(row >= total_steps, row - total_steps, row)
        slot = jnp.floor((row + 0.5) / steps)
        owner = tm.astype(f32) - slot
        owner = jnp.where(owner < 0, owner + groups, owner)
        return row + steps * (owner - slot)

    shape = (2 * total_steps, total_steps)
    mask[...] = jnp.where(times(shape, 1) <= times(shape, 0), 0.0, negative_floor)

    for load in loads[1:5]:
        load.wait()
    batch = 4
    for g in range(groups // batch):
        for k in range(g * batch, (g + 1) * batch):
            if k:
                first[k - 1].wait_recv()
        there = pl.ds(g * batch * rows, batch * rows)
        flat = normed(recv1[g * batch:(g + 1) * batch].reshape(batch * rows, 512).astype(f32))
        for target, weight, scale in ((qf, wqt, 0.125), (kf, wkt, None), (vf, wvt, None)):
            result = mm(flat, weight[...])
            if scale is not None:
                result = result * scale
            for h in range(pairs):
                target[h, there, :] = result[:, h * 128:(h + 1) * 128]

    def one_agent(a, carry):
        mine = pl.ds(a, total_steps, stride=sub)
        for h in range(pairs):
            query = two_heads(qf[h, mine, :].astype(bf16))
            scores = mm_nt(query, kf[h, mine, :].astype(bf16)) + mask[...]
            weights = jnp.exp(scores - jnp.max(scores, axis=-1, keepdims=True))
            totals = jnp.sum(weights, axis=-1, keepdims=True)
            summed = mm(weights.astype(bf16), vf[h, mine, :].astype(bf16))
            mixed_t[h, mine, :] = join_heads(summed / totals)
        return carry

    lax.fori_loop(0, sub, one_agent, 0)

    second = []
    for k in list(range(1, groups)) + [0]:
        piece = jnp.concatenate([mixed_t[h, pl.ds(k * rows, rows), :] for h in range(pairs)], axis=1).astype(bf16)
        if k == 0:
            recv2[0] = piece
            continue
        send2[k] = piece
        copy = pltpu.make_async_remote_copy(
            src_ref=send2.at[k], dst_ref=recv2.at[k], send_sem=s2.at[k], recv_sem=r2.at[k],
            device_id={"tm": tm_peer(-k)}, device_id_type=MESH,
        )
        copy.start()
        second.append(copy)

    loads[5].wait()
    for g in range(groups // batch):
        for k in range(g * batch, (g + 1) * batch):
            if k:
                second[k - 1].wait_recv()
        added = mm(recv2[g * batch:(g + 1) * batch].reshape(batch * rows, 512), wot[...])
        for k in range(batch):
            base = pl.multiple_of(tm_peer(g * batch + k) * sub, sub)
            for t in range(steps):
                after[t, pl.ds(base, sub), :] = added[(k * steps + t) * sub:(k * steps + t + 1) * sub]
    for t in range(steps):
        both = (wide[t] + after[t]).astype(bf16)
        aft_b[t] = both
        tokens[t] = normed(both.astype(f32))

    third = []

    def send_tokens(target, step, chip, part, j):
        for c in range(2):
            here = pl.ds(c * half, half)
            source = tokens.at[step, here, :]
            destination = target.at[ag, here, :]
            local_copy = pltpu.make_async_copy(source, destination, r3.at[part, ag])
            copy = pltpu.make_async_remote_copy(
                src_ref=source, dst_ref=destination, send_sem=s3.at[part, j, c], recv_sem=r3.at[part, ag],
                device_id={"tm": tm - core + c, "agent": chip}, device_id_type=MESH,
            )
            stays = jnp.logical_and(chip == ag, core == c)
            pl.when(stays)(local_copy.start)
            pl.when(jnp.logical_not(stays))(copy.start)
            third.append((stays, copy))

    for j in range(4):
        step = lax.rem(duo + j, 4)
        send_tokens(all_full, step, 2 * step + core, 0, j)
    for j in range(4):
        turn = lax.rem(ag + j, 4)
        send_tokens(all_part, 4 + turn // 2, 4 * core + turn, 1, j)

    fourth = []
    partner = tm + 1 - 2 * core
    full_order = [2 * lax.rem(full_step - j + 4, 4) + e for j in range(4) for e in range(2)]
    part_order = [lax.rem(ag - j + blocks, 4) + 4 * e for j in range(4) for e in range(2)]

    def hand_over(target, part, order):
        handed = []
        for n, source in enumerate(order):
            here = target.at[source, pl.ds(core * half, half), :]
            pltpu.make_async_copy(here, here, r3.at[part, source]).wait()
            copy = pltpu.make_async_remote_copy(
                src_ref=here, dst_ref=here, send_sem=s4.at[part, n], recv_sem=r4.at[part, n],
                device_id={"tm": partner}, device_id_type=MESH,
            )
            copy.start()
            handed.append(copy)
        fourth.extend(handed)
        return handed

    def project(target, result, weights, order, handed):
        for j in range(4):
            for copy in handed[2 * j:2 * j + 2]:
                copy.wait_recv()
            flat = jnp.concatenate([target[order[2 * j + e]] for e in range(2)], axis=0)
            for n, weight in enumerate(weights):
                made = mm(flat, weight[...])
                if n == 0:
                    made = made * 0.125
                for e in range(2):
                    result[order[2 * j + e], n] = made[e * agents:(e + 1) * agents].astype(bf16)

    fifth = []

    def attention(qkv, ret, many, owner_core, step, lanes, slot, part):
        def one_block(k, carry):
            block = ag_peer(-k)
            near_blocks = [nb_ref[block, j] for j in range(near)]
            for h in range(many):
                columns = slice(h * 128, (h + 1) * 128)
                query = two_heads(qkv[block, 0][:, columns])
                keys = jnp.concatenate([qkv[b, 1][:, columns] for b in near_blocks], axis=0)
                values = jnp.concatenate([qkv[b, 2][:, columns] for b in near_blocks], axis=0)
                scores = mm_nt(query, keys)
                weights = jnp.exp(scores - jnp.max(scores, axis=-1, keepdims=True))
                totals = jnp.sum(weights, axis=-1, keepdims=True)
                summed = mm(weights.astype(bf16), values)
                ret[k, :, columns] = join_heads(summed / totals).astype(bf16)
            return carry

        for k0 in range(0, blocks, 4):
            lax.fori_loop(k0, k0 + 4, one_block, 0)
            for k in range(k0, k0 + 4):
                copy = pltpu.make_async_remote_copy(
                    src_ref=ret.at[k], dst_ref=am.at[step, :, lanes], send_sem=s5.at[part, k],
                    recv_sem=r5.at[step, slot],
                    device_id={"tm": tm - core + owner_core, "agent": ag_peer(-k)}, device_id_type=MESH,
                )
                if k:
                    copy.start()
                    fifth.append((None, copy))
                else:
                    stays = owner_core == core
                    own = pltpu.make_async_copy(ret.at[k], am.at[step, :, lanes], r5.at[step, slot])
                    pl.when(stays)(own.start)
                    pl.when(jnp.logical_not(stays))(copy.start)
                    fifth.append((stays, copy))

    stores = []

    def tail(where):
        for w in where:
            width = 256 if w < 4 else 128
            for slot in range(512 // width):
                target = am.at[w, :, pl.ds(slot * width, width)]
                pltpu.make_async_copy(target, target, r5.at[w, slot]).wait()
        both = jnp.concatenate([am[w] for w in where], axis=0)
        base = jnp.concatenate([aft_b[w] for w in where], axis=0).astype(f32)
        after_agent = (base + mm(both, woa[...])).astype(bf16).astype(f32)
        inner = jax.nn.gelu(mm(normed(after_agent), win[...]), approximate=True).astype(bf16)
        final = (after_agent + mm(inner, wmo[...])).astype(bf16)
        for n, w in enumerate(where):
            outs[w] = final[n * agents:(n + 1) * agents]
            store = pltpu.make_async_copy(outs.at[w], out_hbm.at[w], out_sem.at[w])
            store.start()
            stores.append(store)

    for load in loads[6:12]:
        load.wait()
    handed = hand_over(all_full, 0, full_order)
    project(all_full, qkv_full, (wqa, wka, wva), full_order, handed)
    attention(qkv_full, ret_full, 2, full_core, full_step, full_lanes, core, 0)
    handed = hand_over(all_part, 1, part_order)
    project(all_part, qkv_part, (wqb, wkb, wvb), part_order, handed)
    attention(qkv_part, ret_part, 1, part_core, part_step, part_lanes, side * 2 + core, 1)
    for load in loads[12:]:
        load.wait()
    for w in range(0, steps, 2):
        tail([w, w + 1])

    for copy in first + second + fourth:
        copy.wait_send()
    for stays, copy in third + fifth:
        if stays is None:
            copy.wait_send()
        else:
            pl.when(jnp.logical_not(stays))(copy.wait_send)
    for store in stores:
        store.wait()


def local(
    groups, blocks,
    states, neighbours, w_query_t, w_key_t, w_value_t, w_out_t, w_query_a, w_key_a, w_value_a, w_out_a, w_in, w_mlp_out,
):
    steps, agents, width = states.shape
    hidden = w_in.shape[1]
    rows = steps * (agents // groups)
    total = groups * steps
    square = (width, width)
    anywhere = pl.BlockSpec(memory_space=pl.ANY)
    dma = pltpu.SemaphoreType.DMA
    pieces = pltpu.VMEM((groups, rows, width), bf16)
    by_pair = pltpu.VMEM((width // 128, groups * rows, 128), f32)
    return pl.pallas_call(
        functools.partial(kernel, groups, blocks, steps, agents, neighbours.shape[1]),
        out_shape=jax.ShapeDtypeStruct(states.shape, bf16),
        in_specs=[anywhere] * 12,
        out_specs=anywhere,
        scratch_shapes=[
            pltpu.SMEM(neighbours.shape, jnp.int32),
            pltpu.VMEM(states.shape, bf16),
            pltpu.VMEM(states.shape, f32),
            *[pltpu.VMEM(square, bf16)] * 4,
            *[pltpu.VMEM((width, 256), bf16)] * 3,
            *[pltpu.VMEM((width, 128), bf16)] * 3,
            pltpu.VMEM(square, bf16),
            pltpu.VMEM((width, hidden), bf16),
            pltpu.VMEM((hidden, width), bf16),
            pieces, pieces, by_pair, by_pair, by_pair,
            pltpu.VMEM((2 * total, total), f32),
            by_pair, pieces, pieces,
            pltpu.VMEM(states.shape, f32),
            pltpu.VMEM(states.shape, bf16),
            pltpu.VMEM(states.shape, bf16),
            pltpu.VMEM((blocks, agents, width), bf16),
            pltpu.VMEM((blocks, agents, width), bf16),
            pltpu.VMEM((blocks, 3, agents, 256), bf16),
            pltpu.VMEM((blocks, 3, agents, 128), bf16),
            pltpu.VMEM((blocks, agents, 256), bf16),
            pltpu.VMEM((blocks, agents, 128), bf16),
            pltpu.VMEM(states.shape, bf16),
            pltpu.VMEM(states.shape, bf16),
            dma((15,)), dma((steps,)),
            dma((groups,)), dma((groups,)), dma((groups,)), dma((groups,)),
            dma((2, 4, 2)), dma((2, blocks)),
            dma((2, blocks)), dma((2, blocks)),
            dma((2, blocks)), dma((steps, 4)),
        ],
        compiler_params=pltpu.CompilerParams(
            collective_id=0, has_side_effects=True, vmem_limit_bytes=60 * 1024 * 1024
        ),
    )(states, neighbours, w_query_t, w_key_t, w_value_t, w_out_t, w_query_a, w_key_a, w_value_a, w_out_a, w_in, w_mlp_out)


def solution(mesh):
    placed = (P("tm", "agent", None), P(), P(), P(), P(), P(), P(), P(), P(), P(), P(), P())
    return jax.shard_map(
        functools.partial(local, mesh.shape["tm"], mesh.shape["agent"]),
        mesh=mesh, in_specs=placed, out_specs=P("tm", "agent", None), check_vma=False,
    )
```

time: 96.1 us -> 80.1 us (0.83)
  the two profiles are of different devices: /device:TPU:28 before, /device:TPU:1 now
where the time goes in v2:
time: 80.1 us; the launch traced here: 79.7 us
  Pallas kernels  76.3 us (95%)
  local copies, waits for them, and re-layouts  3.44 us (4%)
    pallas_call x1, Pallas kernels, local(): pl.pallas_call(functools.partial(kernel, groups, blocks, steps, agents, n...  76.3 us
    unnamed x2, local copies, waits for them, and re-layouts  3.44 us

profile of v2, /device:TPU:1, one launch (start us, length us, event | category | flops | bytes accessed | tf_op | source)
XLA Modules:
  0.0 79.7 jit_solution(13275928197758854839)
XLA Ops:
  0.0 1.3 %copy.13.nb_hbm = s32[8,4]{1,0:T(8,128)} copy(s32[8,4]{0,1:T(4,128)} %param.13) | data formatting | bytes 256 | tf_op args[1]
  1.3 76.3 %shard_map.118 = bf16[6,128,512]{2,1,0:T(8,128)(2,1)} custom-call(bf16[6,128,512]{2,1,0:T(8,128)(2,1)} %states_hbm.1, s32[8,4]{1,0:T(8,128)} %copy.13.nb_hbm, bf16[512,512]{1,0:T(8,128)(2,1)} %wqt_hbm.1, bf16[512,512]{1,0:T(8,128)(2,1)} %wkt_hbm.1, bf16[512,512]{1,0:T(8,128)(2,1)} %wvt_hbm.1, bf16[512,512]{1,0:T(8,128)(2,1)} %wot_hbm.1, ...), custom_call_target="tpu_custom_call" | custom-call | tf_op jit(solution)/shard_map/pallas_call | solution.py:325
  77.6 2.1 %copy.15 = bf16[6,128,512]{2,1,0:T(8,128)(2,1)} copy(bf16[6,128,512]{2,1,0:T(8,128)(2,1)} %shard_map.118) | data formatting | bytes 1572864

commit v3 on v2

--- a/solution.py
+++ b/solution.py
@@ -11,6 +11,8 @@
 HEADS = 8
 epsilon = 1e-06
 negative_floor = -1e30
+FAR = [1, 2, 3, 4, 5, 6, 7]
+THROTTLE = True
 bf16 = jnp.bfloat16
 f32 = jnp.float32
 
@@ -42,11 +44,11 @@
 def kernel(
     groups, blocks, steps, agents, near,
     states_hbm, nb_hbm, wqt_hbm, wkt_hbm, wvt_hbm, wot_hbm, wqa_hbm, wka_hbm, wva_hbm, woa_hbm, win_hbm, wmo_hbm,
-    out_hbm,
+    outs,
     nb_ref, states, wide, wqt, wkt, wvt, wot, wqa, wka, wva, wqb, wkb, wvb, woa, win, wmo,
     send1, recv1, qf, kf, vf, mask, mixed_t, send2, recv2, after, aft_b, tokens, all_full, all_part,
-    qkv_full, qkv_part, ret_full, ret_part, am, outs,
-    in_sem, out_sem, s1, r1, s2, r2, s3, r3, s4, r4, s5, r5,
+    qkv_full, qkv_part, ret_full, ret_part, am,
+    in_sem, s1, r1, s2, r2, s3, r3, s4, r4, s5, r5,
 ):
     tm = lax.axis_index("tm")
     ag = lax.axis_index("agent")
@@ -56,8 +58,14 @@
     pairs = HEADS // 2
     half = agents // 2
 
+    chips = groups // 2
+    chip = tm // 2
+
     def tm_peer(k):
         return lax.rem(tm + k + groups, groups)
+
+    def chip_at(k):
+        return lax.rem(chip + k + chips, chips)
 
     def ag_peer(k):
         return lax.rem(ag + k + blocks, blocks)
@@ -87,22 +95,40 @@
 
     loads[0].wait()
     wide[...] = states[...].astype(f32)
-    for k in range(groups):
-        base = pl.multiple_of(tm_peer(k) * sub, sub)
-        piece = jnp.concatenate([wide[t, pl.ds(base, sub), :] for t in range(steps)], axis=0).astype(bf16)
-        if k == 0:
-            recv1[0] = piece
-        else:
-            send1[k] = piece
+
+    def share(chip_of, c):
+        return pl.multiple_of((c * chips + chip_of) * sub, sub)
+
+    for q in range(chips):
+        for c in range(2):
+            base = share(chip_at(q), c)
+            send1[2 * q + c] = jnp.concatenate(
+                [wide[t, pl.ds(base, sub), :] for t in range(steps)], axis=0
+            ).astype(bf16)
+    recv1[core] = send1[core]
     pl.semaphore_wait(barrier, groups - 1 + 2 * (blocks - 1))
-    first = []
-    for k in range(1, groups):
-        copy = pltpu.make_async_remote_copy(
-            src_ref=send1.at[k], dst_ref=recv1.at[k], send_sem=s1.at[k], recv_sem=r1.at[k],
-            device_id={"tm": tm_peer(k)}, device_id_type=MESH,
+
+    def to_time(q, c):
+        return pltpu.make_async_remote_copy(
+            src_ref=send1.at[2 * q + c], dst_ref=recv1.at[2 * q + core], send_sem=s1.at[2 * q + c],
+            recv_sem=r1.at[2 * q + core], device_id={"tm": 2 * chip_at(q) + c}, device_id_type=MESH,
         )
+
+    early = [to_time(q, 0) for q in FAR]
+    late = [to_time(q, 1) for q in FAR]
+    beside = to_time(0, 1 - core)
+    for copy in early:
         copy.start()
-        first.append(copy)
+    beside.start()
+    for ahead, copy in zip(early, late):
+        if THROTTLE:
+            ahead.wait_send()
+        copy.start()
+    unsent = late + [beside] + ([] if THROTTLE else early)
+
+    def arrived(buffer, sems, slot):
+        piece = buffer.at[slot]
+        pltpu.make_async_copy(piece, piece, sems.at[slot]).wait()
 
     total_steps = groups * steps
 
@@ -110,9 +136,10 @@
         row = lax.broadcasted_iota(jnp.int32, shape, axis).astype(f32)
         row = jnp.where(row >= total_steps, row - total_steps, row)
         slot = jnp.floor((row + 0.5) / steps)
-        owner = tm.astype(f32) - slot
-        owner = jnp.where(owner < 0, owner + groups, owner)
-        return row + steps * (owner - slot)
+        back = jnp.floor((slot + 0.5) / 2)
+        owner = chip.astype(f32) - back
+        owner = jnp.where(owner < 0, owner + chips, owner)
+        return row + 2 * steps * (owner - back)
 
     shape = (2 * total_steps, total_steps)
     mask[...] = jnp.where(times(shape, 1) <= times(shape, 0), 0.0, negative_floor)
@@ -121,9 +148,10 @@
         load.wait()
     batch = 4
     for g in range(groups // batch):
-        for k in range(g * batch, (g + 1) * batch):
-            if k:
-                first[k - 1].wait_recv()
+        if g == 0:
+            arrived(recv1, r1, 1 - core)
+        for k in range(max(2, g * batch), (g + 1) * batch):
+            arrived(recv1, r1, k)
         there = pl.ds(g * batch * rows, batch * rows)
         flat = normed(recv1[g * batch:(g + 1) * batch].reshape(batch * rows, 512).astype(f32))
         for target, weight, scale in ((qf, wqt, 0.125), (kf, wkt, None), (vf, wvt, None)):
@@ -146,96 +174,110 @@
 
     lax.fori_loop(0, sub, one_agent, 0)
 
-    second = []
-    for k in list(range(1, groups)) + [0]:
-        piece = jnp.concatenate([mixed_t[h, pl.ds(k * rows, rows), :] for h in range(pairs)], axis=1).astype(bf16)
-        if k == 0:
-            recv2[0] = piece
-            continue
-        send2[k] = piece
+    def result_of(slot):
+        return jnp.concatenate([mixed_t[h, pl.ds(slot * rows, rows), :] for h in range(pairs)], axis=1).astype(bf16)
+
+    def to_owner(q, c):
+        return pltpu.make_async_remote_copy(
+            src_ref=send2.at[2 * q + c], dst_ref=recv2.at[core * chips + q], send_sem=s2.at[2 * q + c],
+            recv_sem=r2.at[core * chips + q], device_id={"tm": 2 * chip_at(-q) + c}, device_id_type=MESH,
+        )
+
+    for q in FAR + [0]:
+        for c in range(2):
+            send2[2 * q + c] = result_of(2 * q + c)
+            if q:
+                copy = to_owner(q, c)
+                copy.start()
+                unsent.append(copy)
+    copy = to_owner(0, 1 - core)
+    copy.start()
+    unsent.append(copy)
+    recv2[core * chips] = send2[core]
+
+    maybe = []
+
+    def send_tokens(target, step, to_chip, part, j, c):
+        here = pl.ds(c * half, half)
+        source = tokens.at[step, here, :]
+        destination = target.at[ag, here, :]
+        local_copy = pltpu.make_async_copy(source, destination, r3.at[part, ag])
         copy = pltpu.make_async_remote_copy(
-            src_ref=send2.at[k], dst_ref=recv2.at[k], send_sem=s2.at[k], recv_sem=r2.at[k],
-            device_id={"tm": tm_peer(-k)}, device_id_type=MESH,
+            src_ref=source, dst_ref=destination, send_sem=s3.at[part, j, c], recv_sem=r3.at[part, ag],
+            device_id={"tm": tm - core + c, "agent": to_chip}, device_id_type=MESH,
         )
-        copy.start()
-        second.append(copy)
+        stays = jnp.logical_and(to_chip == ag, core == c)
+        pl.when(stays)(local_copy.start)
+        pl.when(jnp.logical_not(stays))(copy.start)
+        maybe.append((stays, copy))
 
     loads[5].wait()
-    for g in range(groups // batch):
-        for k in range(g * batch, (g + 1) * batch):
-            if k:
-                second[k - 1].wait_recv()
-        added = mm(recv2[g * batch:(g + 1) * batch].reshape(batch * rows, 512), wot[...])
-        for k in range(batch):
-            base = pl.multiple_of(tm_peer(g * batch + k) * sub, sub)
+    for c in range(2):
+        for q in range(1, chips):
+            arrived(recv2, r2, c * chips + q)
+
+        @pl.when(core != c)
+        def _():
+            arrived(recv2, r2, c * chips)
+
+        added = mm(recv2[c * chips:(c + 1) * chips].reshape(chips * rows, 512), wot[...])
+        for q in range(chips):
+            base = share(chip_at(q), c)
             for t in range(steps):
-                after[t, pl.ds(base, sub), :] = added[(k * steps + t) * sub:(k * steps + t + 1) * sub]
-    for t in range(steps):
-        both = (wide[t] + after[t]).astype(bf16)
-        aft_b[t] = both
-        tokens[t] = normed(both.astype(f32))
-
-    third = []
-
-    def send_tokens(target, step, chip, part, j):
-        for c in range(2):
-            here = pl.ds(c * half, half)
-            source = tokens.at[step, here, :]
-            destination = target.at[ag, here, :]
-            local_copy = pltpu.make_async_copy(source, destination, r3.at[part, ag])
-            copy = pltpu.make_async_remote_copy(
-                src_ref=source, dst_ref=destination, send_sem=s3.at[part, j, c], recv_sem=r3.at[part, ag],
-                device_id={"tm": tm - core + c, "agent": chip}, device_id_type=MESH,
-            )
-            stays = jnp.logical_and(chip == ag, core == c)
-            pl.when(stays)(local_copy.start)
-            pl.when(jnp.logical_not(stays))(copy.start)
-            third.append((stays, copy))
-
-    for j in range(4):
-        step = lax.rem(duo + j, 4)
-        send_tokens(all_full, step, 2 * step + core, 0, j)
-    for j in range(4):
-        turn = lax.rem(ag + j, 4)
-        send_tokens(all_part, 4 + turn // 2, 4 * core + turn, 1, j)
-
-    fourth = []
+                after[t, pl.ds(base, sub), :] = added[(q * steps + t) * sub:(q * steps + t + 1) * sub]
+        here = pl.ds(c * half, half)
+        for t in range(steps):
+            both = (wide[t, here, :] + after[t, here, :]).astype(bf16)
+            aft_b[t, here, :] = both
+            tokens[t, here, :] = normed(both.astype(f32))
+        for j in range(4):
+            step = lax.rem(duo + j, 4)
+            send_tokens(all_full, step, 2 * step + core, 0, j, c)
+        for j in range(4):
+            turn = lax.rem(ag + j, 4)
+            send_tokens(all_part, 4 + turn // 2, 4 * core + turn, 1, j, c)
+
     partner = tm + 1 - 2 * core
     full_order = [2 * lax.rem(full_step - j + 4, 4) + e for j in range(4) for e in range(2)]
     part_order = [lax.rem(ag - j + blocks, 4) + 4 * e for j in range(4) for e in range(2)]
 
-    def hand_over(target, part, order):
-        handed = []
-        for n, source in enumerate(order):
-            here = target.at[source, pl.ds(core * half, half), :]
-            pltpu.make_async_copy(here, here, r3.at[part, source]).wait()
-            copy = pltpu.make_async_remote_copy(
-                src_ref=here, dst_ref=here, send_sem=s4.at[part, n], recv_sem=r4.at[part, n],
-                device_id={"tm": partner}, device_id_type=MESH,
-            )
-            copy.start()
-            handed.append(copy)
-        fourth.extend(handed)
-        return handed
-
-    def project(target, result, weights, order, handed):
-        for j in range(4):
-            for copy in handed[2 * j:2 * j + 2]:
-                copy.wait_recv()
-            flat = jnp.concatenate([target[order[2 * j + e]] for e in range(2)], axis=0)
+    def hand_over(target, part, source, rows_of):
+        here = target.at[source, pl.ds(rows_of * half, half), :]
+        return pltpu.make_async_remote_copy(
+            src_ref=here, dst_ref=here, send_sem=s4.at[part, source], recv_sem=r4.at[part, source],
+            device_id={"tm": partner}, device_id_type=MESH,
+        )
+
+    def project(target, part, order, c, result, weights):
+        here = pl.ds(c * half, half)
+        for j in range(0, blocks, 4):
+            for source in order[j:j + 4]:
+                copy = hand_over(target, part, source, c)
+
+                @pl.when(core == c)
+                def _():
+                    piece = target.at[source, here, :]
+                    pltpu.make_async_copy(piece, piece, r3.at[part, source]).wait()
+                    copy.start()
+
+                @pl.when(core != c)
+                def _():
+                    copy.wait_recv()
+
+            flat = jnp.concatenate([target[source, here, :] for source in order[j:j + 4]], axis=0)
             for n, weight in enumerate(weights):
                 made = mm(flat, weight[...])
                 if n == 0:
                     made = made * 0.125
-                for e in range(2):
-                    result[order[2 * j + e], n] = made[e * agents:(e + 1) * agents].astype(bf16)
+                for e, source in enumerate(order[j:j + 4]):
+                    result[source, n, here, :] = made[e * half:(e + 1) * half].astype(bf16)
 
     fifth = []
 
     def attention(qkv, ret, many, owner_core, step, lanes, slot, part):
         def one_block(k, carry):
             block = ag_peer(-k)
-            near_blocks = [nb_ref[block, j] for j in range(near)]
+            near_blocks = [nb_ref[j, block] for j in range(near)]
             for h in range(many):
                 columns = slice(h * 128, (h + 1) * 128)
                 query = two_heads(qkv[block, 0][:, columns])
@@ -266,8 +308,6 @@
                     pl.when(jnp.logical_not(stays))(copy.start)
                     fifth.append((stays, copy))
 
-    stores = []
-
     def tail(where):
         for w in where:
             width = 256 if w < 4 else 128
@@ -281,32 +321,32 @@
         final = (after_agent + mm(inner, wmo[...])).astype(bf16)
         for n, w in enumerate(where):
             outs[w] = final[n * agents:(n + 1) * agents]
-            store = pltpu.make_async_copy(outs.at[w], out_hbm.at[w], out_sem.at[w])
-            store.start()
-            stores.append(store)
 
     for load in loads[6:12]:
         load.wait()
-    handed = hand_over(all_full, 0, full_order)
-    project(all_full, qkv_full, (wqa, wka, wva), full_order, handed)
+    of_full = (all_full, 0, full_order)
+    of_part = (all_part, 1, part_order)
+    project(*of_full, 0, qkv_full, (wqa, wka, wva))
+    project(*of_part, 0, qkv_part, (wqb, wkb, wvb))
+    project(*of_full, 1, qkv_full, (wqa, wka, wva))
     attention(qkv_full, ret_full, 2, full_core, full_step, full_lanes, core, 0)
-    handed = hand_over(all_part, 1, part_order)
-    project(all_part, qkv_part, (wqb, wkb, wvb), part_order, handed)
+    project(*of_part, 1, qkv_part, (wqb, wkb, wvb))
     attention(qkv_part, ret_part, 1, part_core, part_step, part_lanes, side * 2 + core, 1)
     for load in loads[12:]:
         load.wait()
     for w in range(0, steps, 2):
         tail([w, w + 1])
 
-    for copy in first + second + fourth:
+    for copy in unsent:
         copy.wait_send()
-    for stays, copy in third + fifth:
+    for source in range(blocks):
+        for part, target in ((0, all_full), (1, all_part)):
+            hand_over(target, part, source, core).wait_send()
+    for stays, copy in maybe + fifth:
         if stays is None:
             copy.wait_send()
         else:
             pl.when(jnp.logical_not(stays))(copy.wait_send)
-    for store in stores:
-        store.wait()
 
 
 def local(
@@ -324,11 +364,11 @@
     by_pair = pltpu.VMEM((width // 128, groups * rows, 128), f32)
     return pl.pallas_call(
         functools.partial(kernel, groups, blocks, steps, agents, neighbours.shape[1]),
-        out_shape=jax.ShapeDtypeStruct(states.shape, bf16),
+        out_shape=pltpu.VMEM(states.shape, bf16),
         in_specs=[anywhere] * 12,
-        out_specs=anywhere,
+        out_specs=pl.BlockSpec(memory_space=pltpu.VMEM),
         scratch_shapes=[
-            pltpu.SMEM(neighbours.shape, jnp.int32),
+            pltpu.SMEM(neighbours.shape[::-1], jnp.int32),
             pltpu.VMEM(states.shape, bf16),
             pltpu.VMEM(states.shape, f32),
             *[pltpu.VMEM(square, bf16)] * 4,
@@ -350,8 +390,7 @@
             pltpu.VMEM((blocks, agents, 256), bf16),
             pltpu.VMEM((blocks, agents, 128), bf16),
             pltpu.VMEM(states.shape, bf16),
-            pltpu.VMEM(states.shape, bf16),
-            dma((15,)), dma((steps,)),
+            dma((15,)),
             dma((groups,)), dma((groups,)), dma((groups,)), dma((groups,)),
             dma((2, 4, 2)), dma((2, blocks)),
             dma((2, blocks)), dma((2, blocks)),
@@ -360,7 +399,7 @@
         compiler_params=pltpu.CompilerParams(
             collective_id=0, has_side_effects=True, vmem_limit_bytes=60 * 1024 * 1024
         ),
-    )(states, neighbours, w_query_t, w_key_t, w_value_t, w_out_t, w_query_a, w_key_a, w_value_a, w_out_a, w_in, w_mlp_out)
+    )(states, neighbours.T, w_query_t, w_key_t, w_value_t, w_out_t, w_query_a, w_key_a, w_value_a, w_out_a, w_in, w_mlp_out)
 
 
 def solution(mesh):

time: 80.1 us -> 71.2 us (0.89)
  Pallas kernels: 76.3 us -> 70.1 us
  local copies, waits for them, and re-layouts: 3.44 us -> 0.88 us
    pallas_call x1, Pallas kernels: 76.3 us -> 70.1 us  [local(): pl.pallas_call(functools.partial(kernel, groups, blocks, steps, agents, n...]
    unnamed x2 -> x1, local copies, waits for them, and re-layouts: 3.44 us -> 0.88 us
where the time goes in v3:
time: 71.2 us; the launch traced here: 71 us
  Pallas kernels  70.1 us (98%)
  local copies, waits for them, and re-layouts  0.88 us (1%)
    pallas_call x1, Pallas kernels, local(): pl.pallas_call(functools.partial(kernel, groups, blocks, steps, agents, n...  70.1 us

profile of v3, /device:TPU:1, one launch (start us, length us, event | category | flops | bytes accessed | tf_op | source)
XLA Modules:
  0.0 71.0 jit_solution(15457663029661425885)
XLA Ops:
  0.0 70.1 %shard_map.118 = bf16[6,128,512]{2,1,0:T(8,128)(2,1)S(1)} custom-call(bf16[6,128,512]{2,1,0:T(8,128)(2,1)} %states_hbm.1, s32[4,8]{1,0:T(4,128)} %bitcast.1, bf16[512,512]{1,0:T(8,128)(2,1)} %wqt_hbm.1, bf16[512,512]{1,0:T(8,128)(2,1)} %wkt_hbm.1, bf16[512,512]{1,0:T(8,128)(2,1)} %wvt_hbm.1, bf16[512,512]{1,0:T(8,128)(2,1)} %wot_hbm.1, ...), custom_call_target="tpu_custom_call" | custom-call | tf_op jit(solution)/shard_map/pallas_call | solution.py:365
  70.1 0.9 %copy.14 = bf16[6,128,512]{2,1,0:T(8,128)(2,1)} copy(bf16[6,128,512]{2,1,0:T(8,128)(2,1)S(1)} %shard_map.118) | data formatting | bytes 1572864

commit v4 on v3

--- a/solution.py
+++ b/solution.py
@@ -11,8 +11,7 @@
 HEADS = 8
 epsilon = 1e-06
 negative_floor = -1e30
-FAR = [1, 2, 3, 4, 5, 6, 7]
-THROTTLE = True
+FAR = [4, 5, 3, 2, 6, 7, 1]
 bf16 = jnp.bfloat16
 f32 = jnp.float32
 
@@ -121,10 +120,9 @@
         copy.start()
     beside.start()
     for ahead, copy in zip(early, late):
-        if THROTTLE:
-            ahead.wait_send()
+        ahead.wait_send()
         copy.start()
-    unsent = late + [beside] + ([] if THROTTLE else early)
+    unsent = late + [beside]
 
     def arrived(buffer, sems, slot):
         piece = buffer.at[slot]
@@ -172,7 +170,7 @@
             mixed_t[h, mine, :] = join_heads(summed / totals)
         return carry
 
-    lax.fori_loop(0, sub, one_agent, 0)
+    lax.fori_loop(0, sub, one_agent, 0, unroll=4)
 
     def result_of(slot):
         return jnp.concatenate([mixed_t[h, pl.ds(slot * rows, rows), :] for h in range(pairs)], axis=1).astype(bf16)
@@ -290,9 +288,9 @@
                 ret[k, :, columns] = join_heads(summed / totals).astype(bf16)
             return carry
 
-        for k0 in range(0, blocks, 4):
-            lax.fori_loop(k0, k0 + 4, one_block, 0)
-            for k in range(k0, k0 + 4):
+        for k0 in range(0, blocks, 2):
+            lax.fori_loop(k0, k0 + 2, one_block, 0, unroll=2)
+            for k in range(k0, k0 + 2):
                 copy = pltpu.make_async_remote_copy(
                     src_ref=ret.at[k], dst_ref=am.at[step, :, lanes], send_sem=s5.at[part, k],
                     recv_sem=r5.at[step, slot],

time: 71.2 us -> 67.1 us (0.942); the launches traced: 71 us -> 66 us
  Pallas kernels: 70.1 us -> 65.1 us
    pallas_call x1, Pallas kernels: 70.1 us -> 65.1 us  [local(): pl.pallas_call(functools.partial(kernel, groups, blocks, steps, agents, n...]
where the time goes in v4:
time: 67.1 us; the launch traced here: 66 us
  Pallas kernels  65.1 us (97%)
  local copies, waits for them, and re-layouts  0.88 us (1%)
    pallas_call x1, Pallas kernels, local(): pl.pallas_call(functools.partial(kernel, groups, blocks, steps, agents, n...  65.1 us

profile of v4, /device:TPU:1, one launch (start us, length us, event | category | flops | bytes accessed | tf_op | source)
XLA Modules:
  0.0 66.0 jit_solution(7754181664595408408)
XLA Ops:
  0.0 65.1 %shard_map.118 = bf16[6,128,512]{2,1,0:T(8,128)(2,1)S(1)} custom-call(bf16[6,128,512]{2,1,0:T(8,128)(2,1)} %states_hbm.1, s32[4,8]{1,0:T(4,128)} %bitcast.1, bf16[512,512]{1,0:T(8,128)(2,1)} %wqt_hbm.1, bf16[512,512]{1,0:T(8,128)(2,1)} %wkt_hbm.1, bf16[512,512]{1,0:T(8,128)(2,1)} %wvt_hbm.1, bf16[512,512]{1,0:T(8,128)(2,1)} %wot_hbm.1, ...), custom_call_target="tpu_custom_call" | custom-call | tf_op jit(solution)/shard_map/pallas_call | solution.py:363
  65.1 0.9 %copy.14 = bf16[6,128,512]{2,1,0:T(8,128)(2,1)} copy(bf16[6,128,512]{2,1,0:T(8,128)(2,1)S(1)} %shard_map.118) | data formatting | bytes 1572864

commit v5 on v4

--- a/solution.py
+++ b/solution.py
@@ -288,7 +288,7 @@
                 ret[k, :, columns] = join_heads(summed / totals).astype(bf16)
             return carry
 
-        for k0 in range(0, blocks, 2):
+        for k0 in (4, 6, 2, 0):
             lax.fori_loop(k0, k0 + 2, one_block, 0, unroll=2)
             for k in range(k0, k0 + 2):
                 copy = pltpu.make_async_remote_copy(

time: 67.1 us -> 66.8 us (level); the launches traced: 66 us -> 66.7 us
  Pallas kernels: 65.1 us -> 65.8 us
    pallas_call x1, Pallas kernels: 65.1 us -> 65.8 us  [local(): pl.pallas_call(functools.partial(kernel, groups, blocks, steps, agents, n...]
where the time goes in v5:
time: 66.8 us; the launch traced here: 66.7 us
  Pallas kernels  65.8 us (99%)
  local copies, waits for them, and re-layouts  0.88 us (1%)
    pallas_call x1, Pallas kernels, local(): pl.pallas_call(functools.partial(kernel, groups, blocks, steps, agents, n...  65.8 us

profile of v5, /device:TPU:1, one launch (start us, length us, event | category | flops | bytes accessed | tf_op | source)
XLA Modules:
  0.0 66.7 jit_solution(11723580823517745238)
XLA Ops:
  0.0 65.8 %shard_map.118 = bf16[6,128,512]{2,1,0:T(8,128)(2,1)S(1)} custom-call(bf16[6,128,512]{2,1,0:T(8,128)(2,1)} %states_hbm.1, s32[4,8]{1,0:T(4,128)} %bitcast.1, bf16[512,512]{1,0:T(8,128)(2,1)} %wqt_hbm.1, bf16[512,512]{1,0:T(8,128)(2,1)} %wkt_hbm.1, bf16[512,512]{1,0:T(8,128)(2,1)} %wvt_hbm.1, bf16[512,512]{1,0:T(8,128)(2,1)} %wot_hbm.1, ...), custom_call_target="tpu_custom_call" | custom-call | tf_op jit(solution)/shard_map/pallas_call | solution.py:363
  65.8 0.9 %copy.14 = bf16[6,128,512]{2,1,0:T(8,128)(2,1)} copy(bf16[6,128,512]{2,1,0:T(8,128)(2,1)S(1)} %shard_map.118) | data formatting | bytes 1572864
